TPU v7x, 128 devices: a whole 4x4x4 slice. The times are simulated.
128 devices in a mesh: branch: 2 (over core), group: 2 (over y_hi), seq: 32 (over y_lo, x, z).
Axes of the slice: x: 4, y: 4 (y_hi: 2, y_lo: 2; y = y_hi * 2 + y_lo), z: 4, core: 2. Of those that a mesh axis runs over, the one named last changes fastest.
Arguments:
- query_rows: bfloat16 [2, 10240, 4096], P('branch', ('group', 'seq')), parts along dimension 1, may hold values from -10 to 10
- key_rows: bfloat16 [2, 10240, 4096], P('branch', ('group', 'seq')), parts along dimension 1, may hold values from -9 to 9
- value_rows: bfloat16 [2, 10240, 4096], P('branch', ('group', 'seq')), parts along dimension 1, may hold values from -80 to 80
- residual: bfloat16 [10240, 2560], P(('group', 'seq')), parts along dimension 0, may hold values from -6 to 6
- control_mask: int32 [10240], P(('group', 'seq')), parts along dimension 0, may hold values 0 or 1
- step_index: int32 [2], P('group'), parts along dimension 0, may hold values from 0 to 49
- step_gates: float32 [50, 2560], replicated, may hold values from 0.1 to 1.9
- out_weight: bfloat16 [2, 4096, 2560], P('branch', None, 'seq'), may hold values from -0.21875 to 0.21875
Outputs:
- block_out: bfloat16 [2, 10240, 2560], P('branch', ('group', 'seq')), parts along dimension 1
There are 2 independent parts, one for each index of `group`. A program takes and returns all parts, laid end to end along the dimension named above; an argument that names none is the same for every part. Nothing has to cross between parts.
All inputs are finite; a program needn't handle non-finite values. No bound on the sum of `control_mask` on one device may be relied on, other than what follows from the above.
Results may differ from a plain program's by a relative error of at most 0.007.
Values may be sent and summed in bfloat16 or wider, within the bound.
A program may use at most 128 MiB of HBM per device.

v0:
```python
import math

import jax
import jax.numpy as jnp
from jax import lax
from jax.sharding import PartitionSpec as P

HEADS = 32


def shifted(value, axis, steps):
    count = lax.axis_size(axis)
    leading, last = (max(0, -steps), min(count, count - steps))
    return lax.ppermute(value, axis, [(source, source + steps) for source in range(leading, last)])


def attend(exchanged):
    query_all, key_all, value_all = exchanged
    query_local = query_all[:, 0]
    key_local = key_all[:, 0]
    value_local = value_all[:, 0]
    total_rows = query_local.shape[0]
    count_heads = query_local.shape[1]
    head_size = query_local.shape[2]
    score_scale = float(head_size) ** (-0.5)
    block_rows = math.gcd(total_rows, 512)
    query_blocks = query_local.reshape(total_rows // block_rows, block_rows, count_heads, head_size)

    def one_block(query_block):
        scores = (
            jnp.einsum("qhd,khd->hqk", query_block, key_local, preferred_element_type=jnp.float32)
            * score_scale
        )
        peak = jnp.max(scores, axis=2, keepdims=True)
        expo = jnp.exp(scores - peak)
        total_sum = jnp.sum(expo, axis=2, keepdims=True)
        probs = expo.astype(jnp.bfloat16)
        attended = jnp.einsum(
            "hqk,khd->qhd", probs, value_local, preferred_element_type=jnp.float32
        )
        attended = attended / jnp.swapaxes(total_sum, 0, 1)
        return attended.astype(jnp.bfloat16)

    result = lax.map(one_block, query_blocks)
    return result.reshape(total_rows, count_heads, head_size)[:, None]


def per_device(
    query_rows, key_rows, value_rows, residual, control_mask, step_index, step_gates, out_weight
):
    tok_rows = query_rows.shape[1]
    groups = lax.axis_size("seq")
    per_group = HEADS // groups
    head_size = query_rows.shape[2] // HEADS
    query_split = query_rows[0].reshape(tok_rows, groups, per_group, head_size)
    key_split = key_rows[0].reshape(tok_rows, groups, per_group, head_size)
    value_split = value_rows[0].reshape(tok_rows, groups, per_group, head_size)
    head_major = attend(
        (
            lax.all_to_all(query_split, "seq", split_axis=1, concat_axis=0, tiled=True),
            lax.all_to_all(key_split, "seq", split_axis=1, concat_axis=0, tiled=True),
            lax.all_to_all(value_split, "seq", split_axis=1, concat_axis=0, tiled=True),
        )
    )
    weight_local = out_weight[0]
    token_major = lax.all_to_all(head_major, "seq", split_axis=0, concat_axis=1, tiled=True)
    token_flat = token_major.reshape(tok_rows, groups * per_group * head_size)
    projected = jnp.dot(
        token_flat,
        lax.all_gather(weight_local, "seq", axis=1, tiled=True),
        preferred_element_type=jnp.float32,
    )
    hint_local = jnp.where(control_mask[:, None] == 1, projected, jnp.zeros_like(projected)).astype(
        jnp.bfloat16
    )
    hint_moved = shifted(hint_local, "branch", 1)
    step_ids = lax.broadcasted_iota(jnp.int32, (step_gates.shape[0], 1), 0)
    gate_row = jnp.sum(
        jnp.where(step_ids == step_index[0], step_gates, jnp.zeros_like(step_gates)), axis=0
    )
    mixed_out = (
        residual.astype(jnp.float32)
        + gate_row[None, :] * projected
        + hint_moved.astype(jnp.float32)
    )
    is_main = lax.axis_index("branch") == 1
    chosen_out = jnp.where(is_main, mixed_out.astype(jnp.bfloat16), hint_local)
    return chosen_out[None]


def solution(mesh):
    placed = (
        P("branch", ("group", "seq"), None),
        P("branch", ("group", "seq"), None),
        P("branch", ("group", "seq"), None),
        P(("group", "seq"), None),
        P(("group", "seq")),
        P("group"),
        P(),
        P("branch", None, "seq"),
    )
    return jax.shard_map(
        per_device,
        mesh=mesh,
        in_specs=placed,
        out_specs=P("branch", ("group", "seq"), None),
        check_vma=False,
    )
```

profile of v0, /device:TPU:1, one launch (start us, length us, event | category | flops | bytes accessed | tf_op | source)
XLA Modules:
  0.0 436.1 jit_solution(3466766197075098123)
XLA Ops:
  10.5 9.9 %all-to-all-start = ((bf16[160,32,1,128]{3,0,2,1:T(8,128)(2,1)}), bf16[160,32,1,128]{3,0,2,1:T(8,128)(2,1)S(1)}, u32[]{:S(2)}, u32[]{:S(2)}) async-start(bf16[160,32,1,128]{3,0,2,1:T(8,128)(2,1)} %copy.23), calls=%async_computation | async-start | bytes 2621440 | tf_op jit(solution)/shard_map/all_to_all | solution.py:60
  22.2 34.8 %all-to-all-done = bf16[160,32,1,128]{3,0,2,1:T(8,128)(2,1)S(1)} async-done(((bf16[160,32,1,128]{3,0,2,1:T(8,128)(2,1)}), bf16[160,32,1,128]{3,0,2,1:T(8,128)(2,1)S(1)}, u32[]{:S(2)}, u32[]{:S(2)}) %all-to-all-start) | async-done | bytes 1310752 | tf_op jit(solution)/shard_map/all_to_all | solution.py:60
  57.0 8.5 %all-to-all-start.1 = ((bf16[160,32,1,128]{3,0,2,1:T(8,128)(2,1)}), bf16[160,32,1,128]{3,0,2,1:T(8,128)(2,1)S(1)}, u32[]{:S(2)}, u32[]{:S(2)}) async-start(bf16[160,32,1,128]{3,0,2,1:T(8,128)(2,1)} %copy.24), calls=%async_computation.1 | async-start | bytes 2621440 | tf_op jit(solution)/shard_map/all_to_all | solution.py:61
  68.7 34.5 %all-to-all-done.1 = bf16[160,32,1,128]{3,0,2,1:T(8,128)(2,1)S(1)} async-done(((bf16[160,32,1,128]{3,0,2,1:T(8,128)(2,1)}), bf16[160,32,1,128]{3,0,2,1:T(8,128)(2,1)S(1)}, u32[]{:S(2)}, u32[]{:S(2)}) %all-to-all-start.1) | async-done | bytes 1310752 | tf_op jit(solution)/shard_map/all_to_all | solution.py:61
  103.2 177.2 %all-to-all-start.2 = ((bf16[160,32,1,128]{3,0,2,1:T(8,128)(2,1)}), bf16[160,32,1,128]{3,0,2,1:T(8,128)(2,1)}, u32[]{:S(2)}, u32[]{:S(2)}) async-start(bf16[160,32,1,128]{3,0,2,1:T(8,128)(2,1)} %copy.25), calls=%async_computation.2 | async-start | bytes 2621440 | tf_op jit(solution)/shard_map/all_to_all | solution.py:62
  280.4 17.1 %all-to-all-done.2 = bf16[160,32,1,128]{3,0,2,1:T(8,128)(2,1)} async-done(((bf16[160,32,1,128]{3,0,2,1:T(8,128)(2,1)}), bf16[160,32,1,128]{3,0,2,1:T(8,128)(2,1)}, u32[]{:S(2)}, u32[]{:S(2)}) %all-to-all-start.2) | async-done | bytes 1310752 | tf_op jit(solution)/shard_map/all_to_all | solution.py:62
  297.4 72.5 %while.10 = (s32[]{:T(128)}, bf16[10,512,1,128]{3,1,2,0:T(8,128)(2,1)}, bf16[10,512,1,128]{3,1,2,0:T(8,128)(2,1)S(1)}, bf16[5120,1,128]{2,0,1:T(8,128)(2,1)S(1)}, bf16[5120,1,128]{2,0,1:T(8,128)(2,1)}, /*index=5*/s32[]{:T(128)}) while((s32[]{:T(128)}, bf16[10,512,1,128]{3,1,2,0:T(8,128)(2,1)}, bf16[10,512,1,128]{3,1,2,0:T(8,128)(2,1)S(1)}, ...), condition=%wide.region_4.5_spmd, body=%wide.region_1.4_spmd.sunk | while | flops 1363278848 | bytes 34351688 | solution.py:44
  300.9 3.8 fusion.49
  308.1 3.8 fusion.49
  315.4 3.8 fusion.49
  322.6 3.8 fusion.49
  329.9 3.8 fusion.49
  337.1 3.8 fusion.49
  344.4 3.8 fusion.49
  351.6 3.8 fusion.49
  358.9 3.8 fusion.49
  366.1 3.8 fusion.49
  370.4 3.0 reduce.4
  374.7 7.0 %all-to-all-start.3 = ((bf16[32,2,10240]{2,1,0:T(2,128)(2,1)}), bf16[32,2,10240]{2,1,0:T(2,128)(2,1)}, u32[]{:S(2)}, u32[]{:S(2)}) async-start(bf16[32,2,10240]{2,1,0:T(2,128)(2,1)} %reshape.45), calls=%async_computation.3 | async-start | bytes 2621440 | tf_op jit(solution)/shard_map/all_to_all | solution.py:66
  381.7 17.2 %all-to-all-done.3 = bf16[32,2,10240]{2,1,0:T(2,128)(2,1)} async-done(((bf16[32,2,10240]{2,1,0:T(2,128)(2,1)}), bf16[32,2,10240]{2,1,0:T(2,128)(2,1)}, u32[]{:S(2)}, u32[]{:S(2)}) %all-to-all-start.3) | async-done | bytes 1310752 | tf_op jit(solution)/shard_map/all_to_all | solution.py:66
  398.8 7.7 %reshape.46 = bf16[5120,1,1,128]{3,2,1,0:T(2,128)(2,1)S(1)} reshape(bf16[32,2,10240]{2,1,0:T(2,128)(2,1)} %all-to-all-done.3) | data formatting | bytes 2621440
  407.3 12.9 %select_convert_fusion = (bf16[160,2560]{1,0:T(8,128)(2,1)}, f32[160,2560]{1,0:T(8,128)S(1)}) fusion(pred[160]{0:T(512)(128)(4,1)S(1)} %broadcast_compare_fusion, bf16[1,4096,2560]{1,2,0:T(8,128)(2,1)} %all-gather.3.cloned.1.call-done, bf16[20,8,32,128]{3,2,1,0:T(8,128)(2,1)S(1)} %bitcast.113), kind=kOutput, calls=%fused_computation.20 | convolution fusion | flops 3355852800 | bytes 24740000 | tf_op jit(solution)/shard_map/dot_general | solution.py:68
  422.3 4.5 %collective-permute-done = bf16[160,2560]{1,0:T(8,128)(2,1)S(1)} collective-permute-done((bf16[160,2560]{1,0:T(8,128)(2,1)}, bf16[160,2560]{1,0:T(8,128)(2,1)S(1)}, u32[]{:S(2)}, u32[]{:S(2)}) %collective-permute-start) | collective-permute-done | bytes 819232 | tf_op jit(solution)/shard_map/ppermute | solution.py:14
  426.8 2.5 fusion.41
  (44 shorter events, 47.4 us)
Async XLA Ops:
  6.5 400.7 %all-gather.3.cloned.1.call-start = ((), (), s32[]{:S(2)}) async-start(), calls=%async_computation.4 | async-start | bytes 21626880 | tf_op jit(solution)/shard_map/all_gather | solution.py:70
  10.5 9.9 %copy-start = (bf16[1,160,4096]{2,1,0:T(8,128)(2,1)S(1)}, bf16[1,160,4096]{2,1,0:T(8,128)(2,1)}, u32[]{:S(2)}) copy-start(bf16[1,160,4096]{2,1,0:T(8,128)(2,1)} %param.11) | copy-start | bytes 3932164
  10.5 46.5 %all-to-all-start = ((bf16[160,32,1,128]{3,0,2,1:T(8,128)(2,1)}), bf16[160,32,1,128]{3,0,2,1:T(8,128)(2,1)S(1)}, u32[]{:S(2)}, u32[]{:S(2)}) async-start(bf16[160,32,1,128]{3,0,2,1:T(8,128)(2,1)} %copy.23), calls=%async_computation | async-start | bytes 2621440 | tf_op jit(solution)/shard_map/all_to_all | solution.py:60
  57.0 46.2 %all-to-all-start.1 = ((bf16[160,32,1,128]{3,0,2,1:T(8,128)(2,1)}), bf16[160,32,1,128]{3,0,2,1:T(8,128)(2,1)S(1)}, u32[]{:S(2)}, u32[]{:S(2)}) async-start(bf16[160,32,1,128]{3,0,2,1:T(8,128)(2,1)} %copy.24), calls=%async_computation.1 | async-start | bytes 2621440 | tf_op jit(solution)/shard_map/all_to_all | solution.py:61
  103.2 194.2 %all-to-all-start.2 = ((bf16[160,32,1,128]{3,0,2,1:T(8,128)(2,1)}), bf16[160,32,1,128]{3,0,2,1:T(8,128)(2,1)}, u32[]{:S(2)}, u32[]{:S(2)}) async-start(bf16[160,32,1,128]{3,0,2,1:T(8,128)(2,1)} %copy.25), calls=%async_computation.2 | async-start | bytes 2621440 | tf_op jit(solution)/shard_map/all_to_all | solution.py:62
  374.7 7.0 %copy-start.2 = (s32[160]{0:T(256)S(1)}, s32[160]{0:T(256)}, u32[]{:S(2)}) copy-start(s32[160]{0:T(256)} %param.14) | copy-start | bytes 1924
  374.7 24.2 %all-to-all-start.3 = ((bf16[32,2,10240]{2,1,0:T(2,128)(2,1)}), bf16[32,2,10240]{2,1,0:T(2,128)(2,1)}, u32[]{:S(2)}, u32[]{:S(2)}) async-start(bf16[32,2,10240]{2,1,0:T(2,128)(2,1)} %reshape.45), calls=%async_computation.3 | async-start | bytes 2621440 | tf_op jit(solution)/shard_map/all_to_all | solution.py:66
  407.3 14.9 %copy-start.1 = (f32[50,2560]{1,0:T(8,128)S(1)}, f32[50,2560]{1,0:T(8,128)}, u32[]{:S(2)}) copy-start(f32[50,2560]{1,0:T(8,128)} %param.16) | copy-start | bytes 1536004
  420.2 6.6 %collective-permute-start = (bf16[160,2560]{1,0:T(8,128)(2,1)}, bf16[160,2560]{1,0:T(8,128)(2,1)S(1)}, u32[]{:S(2)}, u32[]{:S(2)}) collective-permute-start(bf16[160,2560]{1,0:T(8,128)(2,1)} %get-tuple-element.65), channel_id=1, source_target_pairs={{0,64},{1,65},{2,66},{3,67},{4,68},{5,69},{6,70},{7,71},{8,72},{9,... | collective-permute-start | bytes 2457608 | tf_op jit(solution)/shard_map/ppermute | solution.py:14
Sparse Core Ops, SparseCore 0:
  9.0 269.5 all-gather.2
where the time goes:
time: 437 us; the launch traced here: 436 us
  starting transfers between devices  204 us (47%)
  waiting for transfers between devices  109 us (25%)
  matrix products  66.9 us (15%)
  other arithmetic  24.1 us (6%)
  local copies, waits for them, and re-layouts  18.5 us (4%)
  between operations  14.2 us (3%)
    all_to_all x1, starting transfers between devices, per_device(): lax.all_to_all(value_split, 'seq', split_axis=1, concat_axis=0, tiled=True)  177 us
    dot_general x10, matrix products, one_block(): jnp.einsum('hqk,khd->qhd', probs, value_local, preferred_element_type=jnp...  37.9 us
    all_to_all x1, waiting for transfers between devices, per_device(): lax.all_to_all(query_split, 'seq', split_axis=1, concat_axis=0, tiled=True)  34.8 us
    all_to_all x1, waiting for transfers between devices, per_device(): lax.all_to_all(key_split, 'seq', split_axis=1, concat_axis=0, tiled=True)  34.5 us
    reduce_sum x10, other arithmetic, one_block(): total_sum = jnp.sum(expo, axis=2, keepdims=True)  18.5 us
    all_to_all x1, waiting for transfers between devices, per_device(): lax.all_to_all(head_major, 'seq', split_axis=0, concat_axis=1, tiled=True)  17.2 us
    all_to_all x1, waiting for transfers between devices, per_device(): lax.all_to_all(value_split, 'seq', split_axis=1, concat_axis=0, tiled=True)  17.1 us
    dot_general x10, matrix products, one_block(): jnp.einsum('qhd,khd->hqk', query_block, key_local, preferred_element_type...  16 us
  transfers between devices with their start and end apart: 6, of which 5 were waited for; matrix products, arithmetic and copies ran while one was open for 22% of the time, Pallas kernels for 0%

commit v1 on v0

v1 whole, which is shorter than its diff:
```python
import math

import jax
import jax.numpy as jnp
from jax import lax
from jax.experimental import pallas as pl
from jax.experimental.pallas import tpu as pltpu
from jax.sharding import PartitionSpec as P

HEADS = 32
DH = 128
NX = 4
NZ = 4
PLANE = NX * NZ
SEQ = 2 * PLANE
MESH = pl.DeviceIdType.MESH
KEY_CHUNK = 512
OUT_CHUNK = 512
NT = (((1,), (1,)), ((), ()))


def shifted(value, axis, steps):
    count = lax.axis_size(axis)
    leading, last = (max(0, -steps), min(count, count - steps))
    return lax.ppermute(value, axis, [(source, source + steps) for source in range(leading, last)])


def fused_kernel(
    q_hbm, k_hbm, v_hbm, wt_hbm, out_ref,
    q_s, k_s, v_s, s_a, s_b, m_a, m_b, o_s, att, wg, own, sbuf, rbuf,
    qkv_send, qkv_recv, local_sem, w_send, w_recv, a_send, a_recv, r_send, r_recv,
):
    rows = q_hbm.shape[1]
    half = wt_hbm.shape[1] // 2
    cols = wt_hbm.shape[0]
    keys = k_s.shape[0]
    block = 2 * rows
    factor = float(DH) ** -0.5 * math.log2(math.e)
    me = lax.axis_index("seq")
    y = me // PLANE
    x = (me // NZ) % NX
    z = me % NZ

    def index(yy, xx, zz):
        return yy * PLANE + ((xx + NX) % NX) * NZ + (zz + NZ) % NZ

    def aligned(value, step):
        return pl.ds(pl.multiple_of(value * step, step), step)

    def q_slot(source):
        return q_s.at[aligned((source % PLANE) * 2 + source // PLANE, rows)]

    def k_slot(source):
        return k_s.at[aligned(source, rows)]

    def v_slot(source):
        return v_s.at[aligned(source, rows), pl.ds(0, DH)]

    streams = ((q_hbm, q_slot), (k_hbm, k_slot), (v_hbm, v_slot))

    def head_of(hbm, head):
        return hbm.at[0, :, aligned(head, DH)]

    def qkv_copy(number, peer, source):
        hbm, slot = streams[number]
        return pltpu.make_async_remote_copy(
            src_ref=head_of(hbm, peer), dst_ref=slot(source),
            send_sem=qkv_send.at[number, peer], recv_sem=qkv_recv.at[number, source],
            device_id={"seq": peer}, device_id_type=MESH,
        )

    def w_slot(source):
        return wg.at[aligned(source, cols)]

    def w_copy(slot, peer, number):
        return pltpu.make_async_remote_copy(
            src_ref=w_slot(slot), dst_ref=w_slot(slot),
            send_sem=w_send.at[number], recv_sem=w_recv.at[slot],
            device_id={"seq": peer}, device_id_type=MESH,
        )

    def w_wait(slot):
        w_copy(slot, me, 0).wait_recv()

    own_copies = [
        pltpu.make_async_copy(head_of(hbm, me), slot(me), local_sem.at[n])
        for n, (hbm, slot) in enumerate(streams)
    ]
    own_w = pltpu.make_async_copy(wt_hbm.at[:, aligned(y, half)], w_slot(me), local_sem.at[3])
    for copy in own_copies:
        copy.start()
    own_w.start()

    barrier = pltpu.get_barrier_semaphore()

    @pl.loop(1, SEQ)
    def _(k):
        pl.semaphore_signal(
            barrier, inc=1, device_id={"seq": (me + k) % SEQ}, device_id_type=MESH
        )

    pl.semaphore_wait(barrier, SEQ - 1)

    def peer_at(k):
        return ((y + k // PLANE) % 2) * PLANE + ((x + k // NZ) % NX) * NZ + (z + k) % NZ

    for number in range(3):
        @pl.loop(1, SEQ)
        def _(k):
            qkv_copy(number, peer_at(k), me).start()

    partner = (1 - y) * PLANE + x * NZ + z
    w_first = pltpu.make_async_remote_copy(
        src_ref=wt_hbm.at[:, aligned(1 - y, half)], dst_ref=w_slot(me),
        send_sem=w_send.at[0], recv_sem=w_recv.at[me],
        device_id={"seq": partner}, device_id_type=MESH,
    )
    w_first.start()
    v_s[:, DH:] = jnp.ones((keys, DH), jnp.bfloat16)

    def send_w(slot, peer, number):
        w_copy(slot, peer, number).start()

    def flow(kind, along, across):
        return (index(0, x + along, z + across) if kind == 0 else index(1, x + across, z + along))

    def first_peer(kind, step):
        return index(y, x + step, z) if kind == 0 else index(y, x, z + step)

    def second_peer(kind, step):
        return index(y, x, z + step) if kind == 0 else index(y, x + step, z)

    def stage_one():
        for kind in range(2):
            for at, step in enumerate((1, -1, 2)):
                send_w(flow(kind, 0, 0), first_peer(kind, step), 1 + 3 * kind + at)
        for kind in range(2):
            for at, step in enumerate((1, -1)):
                send_w(flow(kind, 0, 0), second_peer(kind, step), 7 + 2 * kind + at)

    def stage_two(along):
        for kind in range(2):
            w_wait(flow(kind, along, 0))
            for at, step in enumerate((1, -1)):
                number = 11 + 4 * (along % NX - 1) + 2 * kind + at
                send_w(flow(kind, along, 0), second_peer(kind, step), number)

    def stage_three(along, step):
        for kind in range(2):
            w_wait(flow(kind, along, -step))
            number = 23 + 2 * (along % NX) + kind
            send_w(flow(kind, along, -step), second_peer(kind, step), number)

    events = {
        3: lambda: stage_two(1),
        4: lambda: stage_two(-1),
        5: lambda: stage_two(2),
        6: lambda: stage_three(0, 1),
        8: lambda: stage_three(1, 1),
        10: lambda: stage_three(-1, -1),
        12: lambda: stage_three(2, -1),
    }

    for number in range(3):
        own_copies[number].wait()

        @pl.loop(1, SEQ)
        def _(k):
            qkv_copy(number, me, (me + k) % SEQ).wait_recv()

    own_w.wait()
    w_wait(partner)
    stage_one()

    def shift_of(step):
        left = PLANE - 1 - step
        return left // NZ, left % NZ

    def plane_at(step):
        dx, dz = shift_of(step)
        return ((x + dx) % NX) * NZ + (z + dz) % NZ

    def attend(step, now, following):
        lanes = KEY_CHUNK // DH
        if following is not None:
            scores_ref, peak_ref = following
            query = q_s[aligned(plane_at(step + 1), block), :]
            peak = None
        if now is not None:
            held_ref, held_peak = now
            total = jnp.zeros((block, 2 * DH), jnp.float32)
        for chunk in range(keys // KEY_CHUNK):
            span = pl.ds(chunk * KEY_CHUNK, KEY_CHUNK)
            if following is not None:
                scores = lax.dot_general(
                    query, k_s[span, :], NT, preferred_element_type=jnp.float32
                )
                scores_ref[:, span] = scores
                for lane in range(lanes):
                    piece = scores[:, lane * DH : (lane + 1) * DH]
                    peak = piece if peak is None else jnp.maximum(peak, piece)
            if now is not None:
                shift = held_peak[...]
                probs = [
                    jnp.exp2(
                        held_ref[:, pl.ds(chunk * KEY_CHUNK + lane * DH, DH)] * factor - shift
                    ).astype(jnp.bfloat16)
                    for lane in range(lanes)
                ]
                total += jnp.dot(
                    jnp.concatenate(probs, axis=1), v_s[span, :],
                    preferred_element_type=jnp.float32,
                )
        if following is not None:
            top = jnp.max(peak, axis=1, keepdims=True) * factor
            peak_ref[...] = jnp.broadcast_to(top, (block, DH))
        if now is not None:
            o_s[step] = (total[:, :DH] / total[:, DH:]).astype(jnp.bfloat16)

    my_plane = x * NZ + z

    def a_copy(step, plane, source):
        return pltpu.make_async_remote_copy(
            src_ref=o_s.at[step], dst_ref=att.at[:, aligned(source, DH)],
            send_sem=a_send.at[step], recv_sem=a_recv.at[source],
            device_id={"seq": y * PLANE + plane}, device_id_type=MESH,
        )

    first, second = (s_a, m_a), (s_b, m_b)
    attend(-1, None, first)

    @pl.loop(0, PLANE // 2 - 1)
    def _(pair):
        for part in range(2):
            step = pair * 2 + part
            for at, event in events.items():
                if at % 2 == part:
                    pl.when(pair == at // 2)(event)
            attend(step, (first, second)[part], (second, first)[part])
            a_copy(step, plane_at(step), my_plane).start()

    attend(PLANE - 2, first, second)
    a_copy(PLANE - 2, plane_at(PLANE - 2), my_plane).start()
    attend(PLANE - 1, second, None)
    own_a = pltpu.make_async_copy(
        o_s.at[PLANE - 1], att.at[:, aligned(my_plane, DH)], local_sem.at[4]
    )
    own_a.start()

    for kind in range(2):
        for along, across in ((-1, -1), (2, -1), (0, 1), (1, 1), (0, 2), (1, 2), (-1, 2), (2, 2)):
            w_wait(flow(kind, along, across))

    @pl.loop(1, PLANE)
    def _(k):
        a_copy(0, my_plane, (my_plane + k) % PLANE).wait_recv()

    own_a.wait()

    def r_copy(chunk):
        return pltpu.make_async_remote_copy(
            src_ref=sbuf.at[chunk], dst_ref=rbuf.at[chunk],
            send_sem=r_send.at[chunk], recv_sem=r_recv.at[chunk],
            device_id={"seq": partner}, device_id_type=MESH,
        )

    chunks = sbuf.shape[0]

    @pl.loop(0, chunks)
    def _(chunk):
        weights = wg[aligned(chunk, OUT_CHUNK), :]
        sbuf[chunk] = lax.dot_general(
            att[aligned(1 - y, rows), :], weights, NT, preferred_element_type=jnp.float32
        ).astype(jnp.bfloat16)
        own[chunk] = lax.dot_general(
            att[aligned(y, rows), :], weights, NT, preferred_element_type=jnp.float32
        )
        r_copy(chunk).start()

    for chunk in range(chunks):
        r_copy(chunk).wait_recv()
        out_ref[:, chunk * OUT_CHUNK : (chunk + 1) * OUT_CHUNK] = own[chunk] + rbuf[
            chunk
        ].astype(jnp.float32)

    for number in range(3):
        @pl.loop(1, SEQ)
        def _(k):
            qkv_copy(number, (me + k) % SEQ, me).wait_send()

    w_first.wait_send()
    for number in range(1, SEQ - 1):
        w_copy(0, me, number).wait_send()

    @pl.loop(0, PLANE - 1)
    def _(step):
        a_copy(step, my_plane, my_plane).wait_send()

    for chunk in range(chunks):
        r_copy(chunk).wait_send()


def per_device(
    query_rows, key_rows, value_rows, residual, control_mask, step_index, step_gates, out_weight
):
    rows = query_rows.shape[1]
    tokens = rows * SEQ
    block = 2 * rows
    width = residual.shape[1]
    features = out_weight.shape[1]
    chunks = width // OUT_CHUNK
    weight_rows = jnp.swapaxes(out_weight[0], 0, 1)
    bf16, f32 = jnp.bfloat16, jnp.float32
    projected = pl.pallas_call(
        fused_kernel,
        out_shape=jax.ShapeDtypeStruct((rows, width), f32),
        in_specs=[pl.BlockSpec(memory_space=pl.ANY)] * 4,
        out_specs=pl.BlockSpec(memory_space=pltpu.VMEM),
        scratch_shapes=[
            pltpu.VMEM((tokens, DH), bf16),
            pltpu.VMEM((tokens, DH), bf16),
            pltpu.VMEM((tokens, 2 * DH), bf16),
            pltpu.VMEM((block, tokens), f32),
            pltpu.VMEM((block, tokens), f32),
            pltpu.VMEM((block, DH), f32),
            pltpu.VMEM((block, DH), f32),
            pltpu.VMEM((PLANE, block, DH), bf16),
            pltpu.VMEM((block, features // 2), bf16),
            pltpu.VMEM((width, features // 2), bf16),
            pltpu.VMEM((chunks, rows, OUT_CHUNK), f32),
            pltpu.VMEM((chunks, rows, OUT_CHUNK), bf16),
            pltpu.VMEM((chunks, rows, OUT_CHUNK), bf16),
            pltpu.SemaphoreType.DMA((3, SEQ)),
            pltpu.SemaphoreType.DMA((3, SEQ)),
            pltpu.SemaphoreType.DMA((5,)),
            pltpu.SemaphoreType.DMA((SEQ,)),
            pltpu.SemaphoreType.DMA((SEQ,)),
            pltpu.SemaphoreType.DMA((PLANE,)),
            pltpu.SemaphoreType.DMA((PLANE,)),
            pltpu.SemaphoreType.DMA((chunks,)),
            pltpu.SemaphoreType.DMA((chunks,)),
        ],
        compiler_params=pltpu.CompilerParams(
            collective_id=0, has_side_effects=True, vmem_limit_bytes=60000 * 1024
        ),
        name="attend_project",
    )(query_rows, key_rows, value_rows, weight_rows)
    hint_local = jnp.where(control_mask[:, None] == 1, projected, jnp.zeros_like(projected)).astype(
        jnp.bfloat16
    )
    hint_moved = shifted(hint_local, "branch", 1)
    step_ids = lax.broadcasted_iota(jnp.int32, (step_gates.shape[0], 1), 0)
    gate_row = jnp.sum(
        jnp.where(step_ids == step_index[0], step_gates, jnp.zeros_like(step_gates)), axis=0
    )
    mixed_out = (
        residual.astype(jnp.float32)
        + gate_row[None, :] * projected
        + hint_moved.astype(jnp.float32)
    )
    is_main = lax.axis_index("branch") == 1
    chosen_out = jnp.where(is_main, mixed_out.astype(jnp.bfloat16), hint_local)
    return chosen_out[None]


def solution(mesh):
    placed = (
        P("branch", ("group", "seq"), None),
        P("branch", ("group", "seq"), None),
        P("branch", ("group", "seq"), None),
        P(("group", "seq"), None),
        P(("group", "seq")),
        P("group"),
        P(),
        P("branch", None, "seq"),
    )
    return jax.shard_map(
        per_device,
        mesh=mesh,
        in_specs=placed,
        out_specs=P("branch", ("group", "seq"), None),
        check_vma=False,
    )
```

time: 437 us -> 166 us (0.38)
  starting transfers between devices: 204 us -> 1.28 us
  Pallas kernels: 0 us -> 155 us
  waiting for transfers between devices: 109 us -> 2.99 us
  matrix products: 66.9 us -> 0 us
  local copies, waits for them, and re-layouts: 18.5 us -> 0.01 us
  other arithmetic: 24.1 us -> 5.85 us
  between operations: 14.2 us -> 0.69 us
    all_to_all x4 -> x0, starting transfers between devices: 202 us -> none  [the longest x1 177 us: per_device(): lax.all_to_all(value_split, 'seq', split_axis=1, concat_axis=0, tiled=True)]
    pallas_call x0 -> x1, Pallas kernels: none -> 155 us  [per_device(): pl.pallas_call(fused_kernel, out_shape=jax.ShapeDtypeStruct((rows, width)...]
    all_to_all x4 -> x0, waiting for transfers between devices: 104 us -> none  [the longest x1 34.8 us: per_device(): lax.all_to_all(query_split, 'seq', split_axis=1, concat_axis=0, tiled=True)]
    dot_general x21 -> x0, matrix products: 66.9 us -> none  [the longest x10 37.9 us: one_block(): jnp.einsum('hqk,khd->qhd', probs, value_local, preferred_element_type=jnp...]
    reduce_sum x10 -> x0, other arithmetic: 18.5 us -> none  [one_block(): total_sum = jnp.sum(expo, axis=2, keepdims=True)]
    unnamed x12 -> x4, local copies, waits for them, and re-layouts: 12.7 us -> 0.01 us
    another operation x4 -> x0, local copies, waits for them, and re-layouts: 5.31 us -> none  [the longest x1 1.61 us: per_device(): query_split = query_rows[0].reshape(tok_rows, groups, per_group, head_size)]
  transfers between devices with their start and end apart: 6 -> 1, of which waited for: 5 -> 1; matrix products, arithmetic and copies ran while one was open for 22% -> 1% of each run, Pallas kernels for 0% -> 0%
where the time goes in v1:
time: 166 us
  Pallas kernels  155 us (93%)
  other arithmetic  5.85 us (4%)
  waiting for transfers between devices  2.99 us (2%)
    pallas_call x1, Pallas kernels, per_device(): pl.pallas_call(fused_kernel, out_shape=jax.ShapeDtypeStruct((rows, width)...  155 us
  transfers between devices with their start and end apart: 1, of which 1 were waited for; matrix products, arithmetic and copies ran while one was open for 1% of the time, Pallas kernels for 0%

profile of v1, /device:TPU:1, one launch (start us, length us, event | category | flops | bytes accessed | tf_op | source)
XLA Modules:
  0.0 165.6 jit_solution(9394580218242037405)
XLA Ops:
  0.0 0.7 broadcast_compare_fusion
  0.7 154.8 %attend_project.1 = f32[160,2560]{1,0:T(8,128)} custom-call(bf16[1,160,4096]{2,1,0:T(8,128)(2,1)} %q_hbm.1, bf16[1,160,4096]{2,1,0:T(8,128)(2,1)} %k_hbm.1, bf16[1,160,4096]{2,1,0:T(8,128)(2,1)} %v_hbm.1, bf16[80,4096]{1,0:T(8,128)(2,1)} %bitcast.7), custom_call_target="tpu_custom_call" | custom-call | tf_op jit(solution)/shard_map/attend_project/pallas_call | solution.py:314
  155.5 0.0 copy-start
  155.5 0.0 copy-start.1
  155.5 2.6 %select_convert_fusion = bf16[160,2560]{1,0:T(8,128)(2,1)} fusion(f32[160,2560]{1,0:T(8,128)} %attend_project.1, pred[160]{0:T(512)(128)(4,1)S(1)} %broadcast_compare_fusion), kind=kLoop, calls=%fused_computation.1 | loop fusion | flops 409600 | bytes 2457760 | tf_op jit(solution)/shard_map/convert_element_type | solution.py:348
  158.1 1.3 collective-permute-start
  160.1 1.2 select_reduce_fusion
  161.3 3.0 %collective-permute-done = bf16[160,2560]{1,0:T(8,128)(2,1)S(1)} collective-permute-done((bf16[160,2560]{1,0:T(8,128)(2,1)}, bf16[160,2560]{1,0:T(8,128)(2,1)S(1)}, u32[]{:S(2)}, u32[]{:S(2)}) %collective-permute-start) | collective-permute-done | bytes 819232 | tf_op jit(solution)/shard_map/ppermute | solution.py:25
  164.3 0.0 copy-done
  164.3 0.0 copy-done.1
  164.3 1.3 fusion.1
  (1 shorter events, 0.0 us)
Async XLA Ops:
  155.5 8.8 %copy-start = (f32[160,2560]{1,0:T(8,128)S(1)}, f32[160,2560]{1,0:T(8,128)}, u32[]{:S(2)}) copy-start(f32[160,2560]{1,0:T(8,128)} %attend_project.1) | copy-start | bytes 4915204
  155.5 8.8 %copy-start.1 = (bf16[160,2560]{1,0:T(8,128)(2,1)S(1)}, bf16[160,2560]{1,0:T(8,128)(2,1)}, u32[]{:S(2)}) copy-start(bf16[160,2560]{1,0:T(8,128)(2,1)} %param.11) | copy-start | bytes 2457604
  158.1 6.1 %collective-permute-start = (bf16[160,2560]{1,0:T(8,128)(2,1)}, bf16[160,2560]{1,0:T(8,128)(2,1)S(1)}, u32[]{:S(2)}, u32[]{:S(2)}) collective-permute-start(bf16[160,2560]{1,0:T(8,128)(2,1)} %select_convert_fusion), channel_id=1, source_target_pairs={{0,64},{1,65},{2,66},{3,67},{4,68},{5,69},{6,70},{7,71},{8,72},{9,... | collective-permute-start | bytes 2457608 | tf_op jit(solution)/shard_map/ppermute | solution.py:25

commit v2 on v1

v2 whole, which is shorter than its diff:
```python
import math

import jax
import jax.numpy as jnp
from jax import lax
from jax.experimental import pallas as pl
from jax.experimental.pallas import tpu as pltpu
from jax.sharding import PartitionSpec as P

DH = 128
NX = 4
NZ = 4
PLANE = NX * NZ
SEQ = 2 * PLANE
MESH = pl.DeviceIdType.MESH
KEY_CHUNK = 512
SPREAD_LAG = 2
RELAY_LAG = 4
W_STEPS = (5, 6, 7, 8, 9, 10, 11, 12, 12, 13)
NT = (((1,), (1,)), ((), ()))


def fused_kernel(
    index_ref, q_hbm, k_hbm, v_hbm, wt_hbm, res_hbm, mask_hbm, gates_hbm, out_ref,
    q_s, k_s, v_s, s_a, s_b, m_a, m_b, o_s, att, wg, sbuf, rbuf, hints, res_s, mask_s, gates_s,
    qkv_send, qkv_recv, local_sem, w_send, w_recv, a_send, a_recv, f_send, g_send,
    r_send, r_recv, h_send, h_recv,
):
    rows = q_hbm.shape[1]
    cols = wt_hbm.shape[0]
    keys = k_s.shape[0]
    block = 2 * rows
    steps = keys // block
    wide = rbuf.shape[3]
    quarter = wt_hbm.shape[1] // 4
    factor = float(DH) ** -0.5 * math.log2(math.e)
    branch = lax.axis_index("branch")
    me = lax.axis_index("seq")
    y = me // PLANE
    x = (me // NZ) % NX
    z = me % NZ

    def index(yy, xx, zz):
        return (yy % 2) * PLANE + ((xx + NX) % NX) * NZ + (zz + NZ) % NZ

    def aligned(value, step):
        return pl.ds(pl.multiple_of(value * step, step), step)

    def q_slot(source):
        order = ((source // PLANE) * NZ + source % NZ) * NX + (source // NZ) % NX
        return q_s.at[aligned(order, rows)]

    def k_slot(source):
        return k_s.at[aligned(source, rows)]

    def v_slot(source):
        return v_s.at[aligned(source, rows), pl.ds(0, DH)]

    streams = ((q_hbm, q_slot), (k_hbm, k_slot), (v_hbm, v_slot))

    def head_of(hbm, head):
        return hbm.at[0, :, aligned(head, DH)]

    def qkv_copy(number, peer, source):
        hbm, slot = streams[number]
        return pltpu.make_async_remote_copy(
            src_ref=head_of(hbm, peer), dst_ref=slot(source),
            send_sem=qkv_send.at[number, peer], recv_sem=qkv_recv.at[number, source],
            device_id={"seq": peer}, device_id_type=MESH,
        )

    def w_slot(yy, zz):
        start = (yy % 2) * wide + (x % 2) * 64 + ((zz + NZ) % NZ) * cols
        return wg.at[pl.ds(pl.multiple_of(start, 16), cols)]

    def w_part(yy, zz, part):
        return w_slot(yy, zz).at[:, pl.ds(part * quarter, quarter)]

    def w_copy(yy, zz, part, peer, number, own=False):
        there = w_part(yy, zz, part)
        here = wt_hbm.at[:, pl.ds(part * quarter, quarter)] if own else there
        return pltpu.make_async_remote_copy(
            src_ref=here, dst_ref=there,
            send_sem=w_send.at[number], recv_sem=w_recv.at[yy % 2, (zz + NZ) % NZ, part],
            device_id={"seq": peer}, device_id_type=MESH,
        )

    def w_wait(yy, zz, part):
        w_copy(yy, zz, part, me, 0).wait_recv()

    local_copies = [
        pltpu.make_async_copy(head_of(hbm, me), slot(me), local_sem.at[n])
        for n, (hbm, slot) in enumerate(streams)
    ] + [
        pltpu.make_async_copy(wt_hbm, w_slot(y, z), local_sem.at[3]),
        pltpu.make_async_copy(res_hbm, res_s, local_sem.at[4]),
        pltpu.make_async_copy(mask_hbm, mask_s, local_sem.at[5]),
        pltpu.make_async_copy(gates_hbm, gates_s, local_sem.at[6]),
    ]
    for copy in local_copies:
        copy.start()

    barrier = pltpu.get_barrier_semaphore()

    @pl.loop(1, SEQ)
    def _(k):
        pl.semaphore_signal(
            barrier, inc=1, device_id={"seq": (me + k) % SEQ}, device_id_type=MESH
        )

    pl.semaphore_signal(barrier, inc=1, device_id={"branch": 1 - branch}, device_id_type=MESH)
    pl.semaphore_wait(barrier, SEQ)

    def peer_at(k):
        return index(y + k // PLANE, x + (k // NZ) % NX, z + k % NZ)

    def offset(step):
        left = 2 * NZ - 1 - step // 2
        return left // NZ, left % NZ

    for number in (1, 2):
        @pl.loop(1, SEQ)
        def _(k):
            qkv_copy(number, peer_at(k), me).start()

    def send_queries(k):
        dy, dz = offset(k // NX * 2)
        qkv_copy(0, index(y + dy, x + k % NX, z + NZ - dz), me).start()

    pl.loop(0, SEQ - NX)(send_queries)
    pl.loop(SEQ - NX + 1, SEQ)(send_queries)

    for at, part in enumerate((2, 3)):
        w_copy(y, z, part, index(y, x, z + 1), 2 * at, True).start()
        w_copy(y, z, part, index(y, x, z - 1), 2 * at + 1, True).start()
        w_copy(y, z, part - 2, index(y + 1, x, z), 4 + at, True).start()
    v_s[:, DH:] = jnp.ones((keys, DH), jnp.bfloat16)
    for yy in range(2):
        spare = pl.multiple_of(yy * wide + (1 - x % 2) * (wide - 64), 64)
        wg[pl.ds(spare, 64), :] = jnp.zeros((64, wg.shape[1]), jnp.bfloat16)

    def along_z(part, other):
        if other:
            w_wait(y + 1, z, part)
        for at, way in enumerate((1, -1)):
            number = 6 + 4 * part + 2 * other + at
            w_copy(y + other, z, part, index(y, x, z + way), number, not other).start()

    def over_y(part, step):
        if step:
            w_wait(y, z + step, part)
        number = 14 + 4 * (part - 2) + step % NZ
        w_copy(y, z + step, part, index(y + 1, x, z), number, step == 0).start()

    def relay_z(part):
        if part < 2:
            for yy, way in enumerate((1, -1)):
                w_wait(yy, z - way, part)
                w_copy(yy, z - way, part, index(y, x, z + way), 22 + 2 * part + yy).start()
        else:
            way = 1 if part == 2 else -1
            w_copy(y, z - way, part, index(y, x, z + way), 24 + part).start()

    actions = (
        lambda: along_z(0, 0),
        lambda: (along_z(0, 1), over_y(2, 0)),
        lambda: (along_z(1, 0), over_y(3, 0)),
        lambda: (over_y(2, -1), relay_z(2), over_y(3, 1), relay_z(3)),
        lambda: along_z(1, 1),
        lambda: (over_y(2, 1), over_y(3, -1)),
        lambda: relay_z(0),
        lambda: relay_z(1),
        lambda: over_y(2, 2),
        lambda: over_y(3, 2),
    )
    events = tuple(zip(W_STEPS, actions))

    def await_queries(step):
        dy, dz = offset(step)
        for tile in range(2):
            source = index(y + dy, 2 * (step % 2) + tile, z + dz)
            pl.when(source != me)(lambda source=source: qkv_copy(0, me, source).wait_recv())

    def attend(step, now, following):
        lanes = KEY_CHUNK // DH
        if following is not None:
            scores_ref, peak_ref = following
            await_queries(step + 1)
            dy, dz = offset(step + 1)
            place = (((y + dy) % 2) * NZ + (z + dz) % NZ) * 2 + (step + 1) % 2
            query = q_s[aligned(place, block), :]
            peak = None
        if now is not None:
            held_ref, held_peak = now
            total = jnp.zeros((block, 2 * DH), jnp.float32)
        for chunk in range(keys // KEY_CHUNK):
            span = pl.ds(chunk * KEY_CHUNK, KEY_CHUNK)
            if following is not None:
                scores = lax.dot_general(
                    query, k_s[span, :], NT, preferred_element_type=jnp.float32
                )
                scores_ref[:, span] = scores
                for lane in range(lanes):
                    piece = scores[:, lane * DH : (lane + 1) * DH]
                    peak = piece if peak is None else jnp.maximum(peak, piece)
            if now is not None:
                shift = held_peak[...]
                probs = [
                    jnp.exp2(
                        held_ref[:, pl.ds(chunk * KEY_CHUNK + lane * DH, DH)] * factor - shift
                    ).astype(jnp.bfloat16)
                    for lane in range(lanes)
                ]
                total += jnp.dot(
                    jnp.concatenate(probs, axis=1), v_s[span, :],
                    preferred_element_type=jnp.float32,
                )
        if following is not None:
            top = jnp.max(peak, axis=1, keepdims=True) * factor
            peak_ref[...] = jnp.broadcast_to(top, (block, DH))
        if now is not None:
            o_s[step] = (total[:, :DH] / total[:, DH:]).astype(jnp.bfloat16)

    def att_part(head, half):
        return att.at[aligned(half, block), aligned(head, DH)]

    def a_copy(head, half, peer, send_sem, source=None):
        part = att_part(head, half)
        return pltpu.make_async_remote_copy(
            src_ref=part if source is None else source, dst_ref=part,
            send_sem=send_sem, recv_sem=a_recv.at[head, half],
            device_id={"seq": peer}, device_id_type=MESH,
        )

    def a_wait(head, half):
        a_copy(head, half, me, a_send.at[0]).wait_recv()

    def deliver(step):
        dy, dz = offset(step)
        peer = index(y + dy, x, z + dz)
        a_copy(me, step % 2, peer, a_send.at[step], o_s.at[step]).start()

    def spread(step):
        dy, dz = offset(step)
        head = index(y + dy, x, z + NZ - dz)
        a_wait(head, step % 2)
        for at, way in enumerate((1, -1)):
            a_copy(head, step % 2, index(y, x + way, z), f_send.at[step, at]).start()

    def spread_own(step):
        for at, way in enumerate((1, -1)):
            a_copy(
                me, step % 2, index(y, x + way, z), f_send.at[step, at], o_s.at[step]
            ).start()

    def relay(step):
        dy, dz = offset(step)
        way = 1 - 2 * (step % 2)
        head = index(y + dy, x - way, z + NZ - dz)
        a_wait(head, step % 2)
        a_copy(head, step % 2, index(y, x + way, z), g_send.at[step]).start()

    first, second = (s_a, m_a), (s_b, m_b)
    local_copies[0].wait()
    for number in (1, 2):
        local_copies[number].wait()

        @pl.loop(1, SEQ)
        def _(k):
            qkv_copy(number, me, (me + k) % SEQ).wait_recv()

        if number == 1:
            attend(-1, None, first)

    @pl.loop(0, steps // 2 - 1)
    def _(pair):
        for part in range(2):
            step = pair * 2 + part
            for at, event in events:
                if at % 2 == part:
                    pl.when(pair == at // 2)(lambda event=event: event() and None)
            attend(step, (first, second)[part], (second, first)[part])
            deliver(step)

            @pl.when(step >= SPREAD_LAG)
            def _():
                spread(step - SPREAD_LAG)

            @pl.when(step >= RELAY_LAG)
            def _():
                relay(step - RELAY_LAG)

    own_parts = [
        pltpu.make_async_copy(
            o_s.at[steps - 2 + half], att_part(me, half), local_sem.at[7 + half]
        )
        for half in range(2)
    ]
    for half in range(2):
        step = steps - 2 + half
        attend(step, (first, second)[half], second if half == 0 else None)
        own_parts[half].start()
        spread_own(step)
        if step - SPREAD_LAG < steps - 2:
            spread(step - SPREAD_LAG)
        relay(step - RELAY_LAG)

    @pl.loop(steps - SPREAD_LAG, steps - 2)
    def _(step):
        spread(step)

    @pl.loop(steps - RELAY_LAG, steps)
    def _(step):
        relay(step)

    for copy in local_copies[3:] + own_parts:
        copy.wait()
    for part in range(2):
        for yy, way in enumerate((1, -1)):
            w_wait(yy, z + way, part)
            w_wait(yy, z + 2, part)
        for step in range(NZ):
            w_wait(y + 1, z + step, part + 2)

    @pl.loop(0, steps)
    def _(step):
        dy, dz = offset(step)
        way = 1 - 2 * (step % 2)
        a_wait(index(y + dy, x + way, z + NZ - dz), step % 2)
        a_wait(index(y + dy, x + 2, z + NZ - dz), step % 2)

    def r_copy(yy, tile, source):
        return pltpu.make_async_remote_copy(
            src_ref=sbuf.at[yy, aligned(tile, rows)], dst_ref=rbuf.at[source, yy],
            send_sem=r_send.at[yy, tile], recv_sem=r_recv.at[yy, source],
            device_id={"seq": index(y, tile, z)}, device_id_type=MESH,
        )

    half_width = out_ref.shape[1] // 2

    def h_copy(yy):
        span = pl.ds(yy * half_width, half_width)
        return pltpu.make_async_remote_copy(
            src_ref=out_ref.at[:, span], dst_ref=hints.at[yy],
            send_sem=h_send.at[yy], recv_sem=h_recv.at[yy],
            device_id={"branch": 1 - branch}, device_id_type=MESH,
        )

    for yy in range(2):
        sbuf[yy] = lax.dot_general(
            att[...], wg[pl.ds(yy * wide, wide), :], NT, preferred_element_type=jnp.float32
        ).astype(jnp.bfloat16)
        for step in (1, 3, 2):
            r_copy(yy, (x + step) % NX, x).start()

    chosen = mask_s[...] == 1
    gate = gates_s[pl.ds(index_ref[0], 1), :]
    low = lax.broadcasted_iota(jnp.int32, (rows, DH), 1) < DH // 2
    for yy in range(2):
        rbuf[x, yy] = sbuf[yy, aligned(x, rows), :]
        for step in (1, 3, 2):
            r_copy(yy, x, (x + step) % NX).wait_recv()
        tiles = []
        for pair in range(NX // 2):
            even = rbuf[2 * pair, yy].astype(jnp.float32)
            odd = rbuf[2 * pair + 1, yy].astype(jnp.float32)
            tiles += [
                even[:, : wide - DH], jnp.where(low, even[:, wide - DH :], odd[:, :DH]),
                odd[:, DH:],
            ]
        projected = jnp.concatenate(tiles, axis=1)
        span = pl.ds(yy * half_width, half_width)

        @pl.when(branch == 0)
        def _():
            out_ref[:, span] = jnp.where(chosen, projected, 0.0).astype(jnp.bfloat16)
            h_copy(yy).start()

        @pl.when(branch == 1)
        def _():
            h_copy(yy).wait_recv()
            out_ref[:, span] = (
                res_s[:, span].astype(jnp.float32)
                + gate[:, yy * half_width : (yy + 1) * half_width] * projected
                + hints[yy].astype(jnp.float32)
            ).astype(jnp.bfloat16)

    for number in range(3):
        @pl.loop(1, SEQ)
        def _(k):
            qkv_copy(number, (me + k) % SEQ, me).wait_send()

    for number in range(28):
        w_copy(0, 0, 0, me, number).wait_send()

    @pl.loop(0, steps - 2)
    def _(step):
        a_copy(0, 0, me, a_send.at[step]).wait_send()

    @pl.loop(0, steps)
    def _(step):
        for at in range(2):
            a_copy(0, 0, me, f_send.at[step, at]).wait_send()
        a_copy(0, 0, me, g_send.at[step]).wait_send()

    for yy in range(2):
        for step in (1, 3, 2):
            r_copy(yy, (x + step) % NX, x).wait_send()

        @pl.when(branch == 0)
        def _():
            h_copy(yy).wait_send()


def per_device(
    query_rows, key_rows, value_rows, residual, control_mask, step_index, step_gates, out_weight
):
    rows = query_rows.shape[1]
    tokens = rows * SEQ
    block = 2 * rows
    steps = tokens // block
    width = residual.shape[1]
    features = out_weight.shape[1]
    wide = NZ * out_weight.shape[2] + 64
    weight_rows = jnp.swapaxes(out_weight[0], 0, 1)
    bf16, f32 = jnp.bfloat16, jnp.float32
    hbm = pl.BlockSpec(memory_space=pl.ANY)
    dma = pltpu.SemaphoreType.DMA
    block_out = pl.pallas_call(
        fused_kernel,
        out_shape=jax.ShapeDtypeStruct((rows, width), bf16),
        in_specs=[pl.BlockSpec(memory_space=pltpu.SMEM)] + [hbm] * 7,
        out_specs=pl.BlockSpec(memory_space=pltpu.VMEM),
        scratch_shapes=[
            pltpu.VMEM((tokens, DH), bf16),
            pltpu.VMEM((tokens, DH), bf16),
            pltpu.VMEM((tokens, 2 * DH), bf16),
            pltpu.VMEM((block, tokens), f32),
            pltpu.VMEM((block, tokens), f32),
            pltpu.VMEM((block, DH), f32),
            pltpu.VMEM((block, DH), f32),
            pltpu.VMEM((steps, block, DH), bf16),
            pltpu.VMEM((NX * rows, features), bf16),
            pltpu.VMEM((2 * wide, features), bf16),
            pltpu.VMEM((2, NX * rows, wide), bf16),
            pltpu.VMEM((NX, 2, rows, wide), bf16),
            pltpu.VMEM((2, rows, width // 2), bf16),
            pltpu.VMEM((rows, width), bf16),
            pltpu.VMEM((rows, 1), jnp.int32),
            pltpu.VMEM(step_gates.shape, f32),
            dma((3, SEQ)), dma((3, SEQ)), dma((9,)), dma((28,)), dma((2, NZ, 4)),
            dma((steps,)), dma((SEQ, 2)), dma((steps, 2)), dma((steps,)),
            dma((2, NX)), dma((2, NX)), dma((2,)), dma((2,)),
        ],
        compiler_params=pltpu.CompilerParams(
            collective_id=0, has_side_effects=True, vmem_limit_bytes=60000 * 1024
        ),
        name="attend_project",
    )(
        step_index, query_rows, key_rows, value_rows, weight_rows, residual,
        control_mask[:, None], step_gates,
    )
    return block_out[None]


def solution(mesh):
    placed = (
        P("branch", ("group", "seq"), None),
        P("branch", ("group", "seq"), None),
        P("branch", ("group", "seq"), None),
        P(("group", "seq"), None),
        P(("group", "seq")),
        P("group"),
        P(),
        P("branch", None, "seq"),
    )
    return jax.shard_map(
        per_device,
        mesh=mesh,
        in_specs=placed,
        out_specs=P("branch", ("group", "seq"), None),
        check_vma=False,
    )
```

time: 166 us -> 144 us (0.87)
  Pallas kernels: 155 us -> 140 us
  other arithmetic: 5.85 us -> 0 us
  local copies, waits for them, and re-layouts: 0.01 us -> 3.52 us
  waiting for transfers between devices: 2.99 us -> 0 us
    pallas_call x1, Pallas kernels: 155 us -> 140 us  [per_device(): pl.pallas_call(fused_kernel, out_shape=jax.ShapeDtypeStruct((rows, width)...]
    ppermute x1 -> x0, waiting for transfers between devices: 2.99 us -> none  [shifted(): lax.ppermute(value, axis, [(source, source + steps) for source in range(l...]
    convert_element_type x1 -> x0, other arithmetic: 2.63 us -> none  [per_device(): jnp.where(control_mask[:, None] == 1, projected, jnp.zeros_like(projected))]
    unnamed x4 -> x1, local copies, waits for them, and re-layouts: 0.01 us -> 2.09 us
  transfers between devices with their start and end apart: 1 -> 0, of which waited for: 1 -> 0; matrix products, arithmetic and copies ran while one was open for 1% -> 0% of each run, Pallas kernels for 0% -> 0%
where the time goes in v2:
time: 144 us
  Pallas kernels  140 us (97%)
  local copies, waits for them, and re-layouts  3.52 us (2%)
    pallas_call x1, Pallas kernels, per_device(): pl.pallas_call(fused_kernel, out_shape=jax.ShapeDtypeStruct((rows, width)...  140 us

profile of v2, /device:TPU:1, one launch (start us, length us, event | category | flops | bytes accessed | tf_op | source)
XLA Modules:
  0.0 144.3 jit_solution(12201269918385293502)
XLA Ops:
  0.7 1.4 copy.9.mask_hbm
  2.1 140.2 %attend_project.1 = bf16[160,2560]{1,0:T(8,128)(2,1)} custom-call(s32[1]{0:T(128)S(6)} %copy.11.index_ref, bf16[1,160,4096]{2,1,0:T(8,128)(2,1)} %q_hbm.1, bf16[1,160,4096]{2,1,0:T(8,128)(2,1)} %k_hbm.1, bf16[1,160,4096]{2,1,0:T(8,128)(2,1)} %v_hbm.1, bf16[80,4096]{1,0:T(8,128)(2,1)} %bitcast.6, bf16[160,2560]{1,0:T(8,128)(2,1)} %res_hbm.1, ...), custom_call_target="tpu_custom_call" | custom-call | tf_op jit(solution)/shard_map/attend_project/pallas_call | solution.py:429
  142.2 2.1 %copy.12 = bf16[1,160,2560]{2,1,0:T(8,128)(2,1)} copy(bf16[1,160,2560]{2,1,0:T(8,128)(2,1)} %bitcast.5) | data formatting | bytes 1638400

commit v3 on v2

--- a/solution.py
+++ b/solution.py
@@ -14,6 +14,7 @@
 SEQ = 2 * PLANE
 MESH = pl.DeviceIdType.MESH
 KEY_CHUNK = 512
+OUT_CHUNK = 256
 SPREAD_LAG = 2
 RELAY_LAG = 4
 W_STEPS = (5, 6, 7, 8, 9, 10, 11, 12, 12, 13)
@@ -31,7 +32,7 @@
     keys = k_s.shape[0]
     block = 2 * rows
     steps = keys // block
-    wide = rbuf.shape[3]
+    wide = rbuf.shape[2] // 2
     quarter = wt_hbm.shape[1] // 4
     factor = float(DH) ** -0.5 * math.log2(math.e)
     branch = lax.axis_index("branch")
@@ -315,6 +316,7 @@
 
     for copy in local_copies[3:] + own_parts:
         copy.wait()
+
     for part in range(2):
         for yy, way in enumerate((1, -1)):
             w_wait(yy, z + way, part)
@@ -329,66 +331,79 @@
         a_wait(index(y + dy, x + way, z + NZ - dz), step % 2)
         a_wait(index(y + dy, x + 2, z + NZ - dz), step % 2)
 
-    def r_copy(yy, tile, source):
+    def part_of(chunk):
+        return pl.ds(chunk * OUT_CHUNK, OUT_CHUNK)
+
+    def r_copy(chunk, tile, source):
         return pltpu.make_async_remote_copy(
-            src_ref=sbuf.at[yy, aligned(tile, rows)], dst_ref=rbuf.at[source, yy],
-            send_sem=r_send.at[yy, tile], recv_sem=r_recv.at[yy, source],
+            src_ref=sbuf.at[aligned(tile, rows), part_of(chunk)],
+            dst_ref=rbuf.at[source, :, part_of(chunk)],
+            send_sem=r_send.at[chunk, tile], recv_sem=r_recv.at[chunk, source],
             device_id={"seq": index(y, tile, z)}, device_id_type=MESH,
         )
 
-    half_width = out_ref.shape[1] // 2
-
-    def h_copy(yy):
-        span = pl.ds(yy * half_width, half_width)
+    chunks = 2 * wide // OUT_CHUNK
+    piece_width = out_ref.shape[1] // 4
+
+    def h_copy(piece):
         return pltpu.make_async_remote_copy(
-            src_ref=out_ref.at[:, span], dst_ref=hints.at[yy],
-            send_sem=h_send.at[yy], recv_sem=h_recv.at[yy],
+            src_ref=out_ref.at[:, pl.ds(piece * piece_width, piece_width)],
+            dst_ref=hints.at[piece],
+            send_sem=h_send.at[piece], recv_sem=h_recv.at[piece],
             device_id={"branch": 1 - branch}, device_id_type=MESH,
         )
 
-    for yy in range(2):
-        sbuf[yy] = lax.dot_general(
-            att[...], wg[pl.ds(yy * wide, wide), :], NT, preferred_element_type=jnp.float32
+    for chunk in range(chunks):
+        sbuf[:, part_of(chunk)] = lax.dot_general(
+            att[...], wg[part_of(chunk), :], NT, preferred_element_type=jnp.float32
         ).astype(jnp.bfloat16)
         for step in (1, 3, 2):
-            r_copy(yy, (x + step) % NX, x).start()
+            r_copy(chunk, (x + step) % NX, x).start()
 
     chosen = mask_s[...] == 1
     gate = gates_s[pl.ds(index_ref[0], 1), :]
+    rbuf[x] = sbuf[aligned(x, rows), :]
     low = lax.broadcasted_iota(jnp.int32, (rows, DH), 1) < DH // 2
     for yy in range(2):
-        rbuf[x, yy] = sbuf[yy, aligned(x, rows), :]
-        for step in (1, 3, 2):
-            r_copy(yy, x, (x + step) % NX).wait_recv()
-        tiles = []
-        for pair in range(NX // 2):
-            even = rbuf[2 * pair, yy].astype(jnp.float32)
-            odd = rbuf[2 * pair + 1, yy].astype(jnp.float32)
-            tiles += [
-                even[:, : wide - DH], jnp.where(low, even[:, wide - DH :], odd[:, :DH]),
-                odd[:, DH:],
-            ]
-        projected = jnp.concatenate(tiles, axis=1)
-        span = pl.ds(yy * half_width, half_width)
-
-        @pl.when(branch == 0)
-        def _():
-            out_ref[:, span] = jnp.where(chosen, projected, 0.0).astype(jnp.bfloat16)
-            h_copy(yy).start()
-
-        @pl.when(branch == 1)
-        def _():
-            h_copy(yy).wait_recv()
-            out_ref[:, span] = (
-                res_s[:, span].astype(jnp.float32)
-                + gate[:, yy * half_width : (yy + 1) * half_width] * projected
-                + hints[yy].astype(jnp.float32)
-            ).astype(jnp.bfloat16)
+        for chunk in (range(2), range(2, chunks))[yy]:
+            for step in (1, 3, 2):
+                r_copy(chunk, x, (x + step) % NX).wait_recv()
+        for pair in range(2):
+            even = rbuf[2 * pair, :, pl.ds(yy * wide, wide)].astype(jnp.float32)
+            odd = rbuf[2 * pair + 1, :, pl.ds(yy * wide, wide)].astype(jnp.float32)
+            projected = jnp.concatenate(
+                [
+                    even[:, : wide - DH], jnp.where(low, even[:, wide - DH :], odd[:, :DH]),
+                    odd[:, DH:],
+                ],
+                axis=1,
+            )
+            piece = 2 * yy + pair
+            start = piece * piece_width
+            span = pl.ds(start, piece_width)
+
+            @pl.when(branch == 0)
+            def _():
+                out_ref[:, span] = jnp.where(chosen, projected, 0.0).astype(jnp.bfloat16)
+                h_copy(piece).start()
+
+            @pl.when(branch == 1)
+            def _():
+                h_copy(piece).wait_recv()
+                out_ref[:, span] = (
+                    res_s[:, span].astype(jnp.float32)
+                    + gate[:, start : start + piece_width] * projected
+                    + hints[piece].astype(jnp.float32)
+                ).astype(jnp.bfloat16)
 
     for number in range(3):
         @pl.loop(1, SEQ)
         def _(k):
             qkv_copy(number, (me + k) % SEQ, me).wait_send()
+
+    for chunk in range(chunks):
+        for step in (1, 3, 2):
+            r_copy(chunk, (x + step) % NX, x).wait_send()
 
     for number in range(28):
         w_copy(0, 0, 0, me, number).wait_send()
@@ -404,12 +419,10 @@
         a_copy(0, 0, me, g_send.at[step]).wait_send()
 
     for yy in range(2):
-        for step in (1, 3, 2):
-            r_copy(yy, (x + step) % NX, x).wait_send()
-
         @pl.when(branch == 0)
         def _():
-            h_copy(yy).wait_send()
+            for pair in range(2):
+                h_copy(2 * yy + pair).wait_send()
 
 
 def per_device(
@@ -442,15 +455,15 @@
             pltpu.VMEM((steps, block, DH), bf16),
             pltpu.VMEM((NX * rows, features), bf16),
             pltpu.VMEM((2 * wide, features), bf16),
-            pltpu.VMEM((2, NX * rows, wide), bf16),
-            pltpu.VMEM((NX, 2, rows, wide), bf16),
-            pltpu.VMEM((2, rows, width // 2), bf16),
+            pltpu.VMEM((NX * rows, 2 * wide), bf16),
+            pltpu.VMEM((NX, rows, 2 * wide), bf16),
+            pltpu.VMEM((4, rows, width // 4), bf16),
             pltpu.VMEM((rows, width), bf16),
             pltpu.VMEM((rows, 1), jnp.int32),
             pltpu.VMEM(step_gates.shape, f32),
             dma((3, SEQ)), dma((3, SEQ)), dma((9,)), dma((28,)), dma((2, NZ, 4)),
             dma((steps,)), dma((SEQ, 2)), dma((steps, 2)), dma((steps,)),
-            dma((2, NX)), dma((2, NX)), dma((2,)), dma((2,)),
+            dma((3, NX)), dma((3, NX)), dma((4,)), dma((4,)),
         ],
         compiler_params=pltpu.CompilerParams(
             collective_id=0, has_side_effects=True, vmem_limit_bytes=60000 * 1024

time: 144 us -> 144 us (level)
  no operation moved by 1% of the time
where the time goes in v3:
time: 144 us
  Pallas kernels  139 us (97%)
  local copies, waits for them, and re-layouts  3.52 us (2%)
    pallas_call x1, Pallas kernels, per_device(): pl.pallas_call(fused_kernel, out_shape=jax.ShapeDtypeStruct((rows, width)...  139 us

profile of v3, /device:TPU:1, one launch (start us, length us, event | category | flops | bytes accessed | tf_op | source)
XLA Modules:
  0.0 143.7 jit_solution(11135405308152062143)
XLA Ops:
  0.7 1.4 copy.9.mask_hbm
  2.1 139.5 %attend_project.1 = bf16[160,2560]{1,0:T(8,128)(2,1)} custom-call(s32[1]{0:T(128)S(6)} %copy.11.index_ref, bf16[1,160,4096]{2,1,0:T(8,128)(2,1)} %q_hbm.1, bf16[1,160,4096]{2,1,0:T(8,128)(2,1)} %k_hbm.1, bf16[1,160,4096]{2,1,0:T(8,128)(2,1)} %v_hbm.1, bf16[80,4096]{1,0:T(8,128)(2,1)} %bitcast.6, bf16[160,2560]{1,0:T(8,128)(2,1)} %res_hbm.1, ...), custom_call_target="tpu_custom_call" | custom-call | tf_op jit(solution)/shard_map/attend_project/pallas_call | solution.py:442
  141.6 2.1 %copy.12 = bf16[1,160,2560]{2,1,0:T(8,128)(2,1)} copy(bf16[1,160,2560]{2,1,0:T(8,128)(2,1)} %bitcast.5) | data formatting | bytes 1638400

commit v4 on v3

--- a/solution.py
+++ b/solution.py
@@ -357,7 +357,7 @@
         sbuf[:, part_of(chunk)] = lax.dot_general(
             att[...], wg[part_of(chunk), :], NT, preferred_element_type=jnp.float32
         ).astype(jnp.bfloat16)
-        for step in (1, 3, 2):
+        for step in (2, 1, 3):
             r_copy(chunk, (x + step) % NX, x).start()
 
     chosen = mask_s[...] == 1
@@ -366,7 +366,7 @@
     low = lax.broadcasted_iota(jnp.int32, (rows, DH), 1) < DH // 2
     for yy in range(2):
         for chunk in (range(2), range(2, chunks))[yy]:
-            for step in (1, 3, 2):
+            for step in (2, 1, 3):
                 r_copy(chunk, x, (x + step) % NX).wait_recv()
         for pair in range(2):
             even = rbuf[2 * pair, :, pl.ds(yy * wide, wide)].astype(jnp.float32)
@@ -402,7 +402,7 @@
             qkv_copy(number, (me + k) % SEQ, me).wait_send()
 
     for chunk in range(chunks):
-        for step in (1, 3, 2):
+        for step in (2, 1, 3):
             r_copy(chunk, (x + step) % NX, x).wait_send()
 
     for number in range(28):

time: 144 us -> 143 us (level)
  no operation moved by 1% of the time
where the time goes in v4:
time: 143 us
  Pallas kernels  139 us (97%)
  local copies, waits for them, and re-layouts  3.52 us (2%)
    pallas_call x1, Pallas kernels, per_device(): pl.pallas_call(fused_kernel, out_shape=jax.ShapeDtypeStruct((rows, width)...  139 us

profile of v4, /device:TPU:1, one launch (start us, length us, event | category | flops | bytes accessed | tf_op | source)
XLA Modules:
  0.0 143.1 jit_solution(17756216192533965448)
XLA Ops:
  0.7 1.4 copy.9.mask_hbm
  2.1 138.9 %attend_project.1 = bf16[160,2560]{1,0:T(8,128)(2,1)} custom-call(s32[1]{0:T(128)S(6)} %copy.11.index_ref, bf16[1,160,4096]{2,1,0:T(8,128)(2,1)} %q_hbm.1, bf16[1,160,4096]{2,1,0:T(8,128)(2,1)} %k_hbm.1, bf16[1,160,4096]{2,1,0:T(8,128)(2,1)} %v_hbm.1, bf16[80,4096]{1,0:T(8,128)(2,1)} %bitcast.6, bf16[160,2560]{1,0:T(8,128)(2,1)} %res_hbm.1, ...), custom_call_target="tpu_custom_call" | custom-call | tf_op jit(solution)/shard_map/attend_project/pallas_call | solution.py:442
  141.0 2.1 %copy.12 = bf16[1,160,2560]{2,1,0:T(8,128)(2,1)} copy(bf16[1,160,2560]{2,1,0:T(8,128)(2,1)} %bitcast.5) | data formatting | bytes 1638400
